TPU v7x, 32 devices: a whole 2x2x4 slice. The times are simulated.
32 devices in a mesh: days: 4 (over y, x), assets: 8 (over z, core).
Axes of the slice: x: 2, y: 2, z: 4, core: 2. Of those that a mesh axis runs over, the one named last changes fastest.
Arguments:
- factors: bfloat16 [768, 256], P('days'), may hold values from -6 to 6
- returns: bfloat16 [768, 16384], P('days', 'assets'), may hold values from -6 to 6
Outputs:
- loadings: float32 [256, 16384], P(None, 'assets')
- covariance: float32 [16384, 16384], P('assets', 'days')
All inputs are finite; a program needn't handle non-finite values.
Results may differ from a plain program's by a relative error of at most 0.0036.
Values may be sent and summed in bfloat16 or wider, within the bound.
No kernel may reach another device: no remote copies, remote signals or barrier semaphores. Data moves between devices by JAX's collectives and lax.ppermute only.
A program may use at most 128 MiB of HBM per device.

v0:
```python
import jax
import jax.numpy as jnp
from jax import lax
from jax.sharding import PartitionSpec as P


def per_device(factors, returns):
    gram = lax.dot_general(
        factors, factors, (((0,), (0,)), ((), ())), preferred_element_type=jnp.float32
    )
    cross = lax.dot_general(
        factors, returns, (((0,), (0,)), ((), ())), preferred_element_type=jnp.float32
    )
    gram, cross = lax.psum((gram, cross), "days")
    lower = jnp.linalg.cholesky(gram)
    middle = lax.linalg.triangular_solve(lower, cross, left_side=True, lower=True)
    loadings = lax.linalg.triangular_solve(
        lower, middle, left_side=True, lower=True, transpose_a=True
    )
    fitted = jnp.dot(factors, loadings.astype(jnp.bfloat16), preferred_element_type=jnp.float32)
    residual = (returns.astype(jnp.float32) - fitted).astype(jnp.bfloat16)
    mine = lax.all_gather(residual, "days", axis=0, tiled=True)
    day_block = lax.all_gather(residual, "assets", axis=1, tiled=True)
    columns = lax.all_to_all(day_block, "days", split_axis=1, concat_axis=0, tiled=True)
    covariance = lax.dot_general(
        mine, columns, (((0,), (0,)), ((), ())), preferred_element_type=jnp.float32
    )
    covariance = covariance / mine.shape[0]
    return (loadings, covariance)


def solution(mesh):
    in_specs = (P("days", None), P("days", "assets"))
    out_specs = (P(None, "assets"), P("assets", "days"))
    return jax.shard_map(
        per_device, mesh=mesh, in_specs=in_specs, out_specs=out_specs, check_vma=False
    )
```

profile of v0, /device:TPU:0, one launch (start us, length us, event | category | flops | bytes accessed | tf_op | source)
XLA Modules:
  0.0 357.5 jit_solution(16672601659228201361)
XLA Ops:
  7.2 0.0 copy-start
  7.2 0.0 all-reduce.4.cloned.1.call-start
  7.2 0.8 copy-done
  8.1 0.9 fusion.15
  9.0 2.9 fusion.16
  11.9 0.0 all-reduce.4.cloned.1.call-update
  11.9 0.0 all-gather.5.cloned.1.call-start
  12.0 76.7 %all-reduce.4.cloned.1.call-done = (f32[256,2048]{1,0:T(8,128)}, f32[256,256]{0,1:T(8,128)}) async-done(((f32[256,2048]{1,0:T(8,128)}, f32[256,256]{0,1:T(8,128)}), (f32[256,2048]{1,0:T(8,128)}, f32[256,256]{0,1:T(8,128)})) %all-reduce.4.cloned.1.call-update) | async-done | bytes 2359312 | tf_op jit(solution)/shard_map/psum | solution.py:14
  88.7 0.0 copy-start.4
  88.7 1.2 copy.7
  89.9 1.0 fusion.5
  90.9 11.7 %cholesky.50 = f32[128,128]{1,0:T(8,128)S(1)} custom-call(f32[128,128]{1,0:T(8,128)S(1)} %cholesky.118), custom_call_target="Cholesky" | custom-call | tf_op jit(solution)/shard_map/jit(cholesky)/cholesky | solution.py:15
  102.7 9.8 %custom-call.16 = f32[1,128,128]{1,2,0:T(8,128)S(1)} custom-call(f32[1,128,128]{2,1,0:T(8,128)S(1)} %get-tuple-element.25), custom_call_target="InvertDiagBlocksLowerTriangular" | custom-call | tf_op jit(solution)/shard_map/jit(cholesky)/cholesky | solution.py:15
  112.5 0.2 constant_dynamic-update-slice_fusion.1
  112.7 0.3 convolution_subtract_fusion.2
  113.0 11.7 %cholesky.105 = f32[128,128]{1,0:T(8,128)S(1)} custom-call(f32[128,128]{1,0:T(8,128)S(1)} %convolution_subtract_fusion.2), custom_call_target="Cholesky" | custom-call | tf_op jit(solution)/shard_map/jit(cholesky)/cholesky | solution.py:15
  124.7 0.6 compare_reduce_fusion
  126.7 0.1 triangular_solve.66
  126.8 4.1 %while.1 = (s32[]{:T(128)}, f32[256,256]{1,0:T(8,128)S(1)}, s32[2,2]{1,0:T(2,128)S(1)}, f32[2,128,128]{2,1,0:T(8,128)S(1)}, s32[]{:T(128)}) while((s32[]{:T(128)}, f32[256,256]{1,0:T(8,128)S(1)}, s32[2,2]{1,0:T(2,128)S(1)}, f32[2,128,128]{2,1,0:T(8,128)S(1)}, s32[]{:T(128)}) %tuple.27), condition=%wide.while_cond, body=%wide.while_body.sunk | while | flops 2 | bytes 131189 | solution.py:17
  126.9 0.6 fusion.32
  127.5 1.4 bitcast_dynamic-update-slice_fusion.2
  129.0 0.6 fusion.32
  129.5 1.4 bitcast_dynamic-update-slice_fusion.2
  130.9 19.7 %custom-call.17 = f32[2,128,128]{1,2,0:T(8,128)S(1)} custom-call(f32[2,128,128]{2,1,0:T(8,128)S(1)} %get-tuple-element.9), custom_call_target="InvertDiagBlocksLowerTriangular" | custom-call | tf_op jit(solution)/shard_map/triangular_solve | solution.py:17
  150.6 0.0 copy-done.4
  150.6 1.1 fusion.2
  151.7 1.0 convolution_subtract_fusion.1
  152.7 1.1 fusion.11
  153.8 1.0 fusion.10
  154.8 1.0 convolution_subtract_fusion
  155.8 1.0 fusion.9
  156.8 0.0 copy-start.3
  156.9 0.1 pad_maximum_fusion
  157.0 1.0 copy-done.3
  158.0 0.0 copy-start.2
  158.0 1.5 fusion.1
  159.5 0.0 all-gather.5.cloned.1.call-update
  159.6 0.0 copy-done.2
  159.6 0.0 all-gather.3.cloned.1.call-start
  159.6 0.7 all-gather.3.cloned.1.call-update
  160.3 64.1 %all-gather.5.cloned.1.call-done = bf16[192,16384]{1,0:T(8,128)(2,1)} async-done(((bf16[192,2048]{1,0:T(8,128)(2,1)}), bf16[192,16384]{1,0:T(8,128)(2,1)}) %all-gather.5.cloned.1.call-update) | async-done | bytes 6291472 | tf_op jit(solution)/shard_map/all_gather | solution.py:23
  224.4 6.3 %copy.12 = bf16[24,4,8,4096]{3,2,0,1:T(8,128)(2,1)} copy(bf16[24,4,8,4096]{3,2,1,0:T(8,128)(2,1)} %bitcast.57) | data formatting | bytes 12582912 | tf_op jit(solution)/shard_map/all_to_all | solution.py:24
  230.7 5.5 %all-to-all-start = ((bf16[192,4,4096]{2,0,1:T(8,128)(2,1)}), bf16[192,4,4096]{2,0,1:T(8,128)(2,1)}, u32[]{:S(2)}, u32[]{:S(2)}) async-start(bf16[192,4,4096]{2,0,1:T(8,128)(2,1)} %bitcast.56), calls=%async_computation | async-start | bytes 12582912 | tf_op jit(solution)/shard_map/all_to_all | solution.py:24
  236.2 90.4 %all-gather.3.cloned.1.call-done = bf16[768,2048]{1,0:T(8,128)(2,1)} async-done(((bf16[192,2048]{1,0:T(8,128)(2,1)}), bf16[768,2048]{1,0:T(8,128)(2,1)}) %all-gather.3.cloned.1.call-update) | async-done | bytes 3145744 | tf_op jit(solution)/shard_map/all_gather | solution.py:22
  326.6 1.8 all-to-all-done
  328.4 0.0 copy-start.1
  328.4 22.6 %convolution_multiply_fusion = f32[2048,4096]{1,0:T(8,128)} fusion(bf16[768,2048]{1,0:T(8,128)(2,1)} %all-gather.3.cloned.1.call-done, bf16[768,4096]{1,0:T(8,128)(2,1)} %bitcast.7), kind=kOutput, calls=%fused_computation.2 | convolution fusion | flops 12893290496 | bytes 42991616 | tf_op jit(solution)/shard_map/dot_general | solution.py:25
  351.0 0.0 copy-done.1
  (9 shorter events, 0.1 us)
Async XLA Ops:
  7.2 0.9 copy-start
  7.2 81.5 %all-reduce.4.cloned.1.call-start = ((), (), s32[]{:S(2)}) async-start(), calls=%async_computation.3 | async-start | bytes 4718592 | tf_op jit(solution)/shard_map/psum | solution.py:14
  11.9 212.5 %all-gather.5.cloned.1.call-start = ((), (), s32[]{:S(2)}) async-start(), calls=%async_computation.2 | async-start | bytes 7077888 | tf_op jit(solution)/shard_map/all_gather | solution.py:23
  88.7 61.9 %copy-start.4 = (f32[256,2048]{1,0:T(8,128)S(1)}, f32[256,2048]{1,0:T(8,128)}, u32[]{:S(2)}) copy-start(f32[256,2048]{1,0:T(8,128)} %get-tuple-element.18) | copy-start | bytes 6291460
  156.8 1.1 copy-start.3
  158.0 1.6 copy-start.2
  159.6 167.1 %all-gather.3.cloned.1.call-start = ((), (), s32[]{:S(2)}) async-start(), calls=%async_computation.1 | async-start | bytes 3932160 | tf_op jit(solution)/shard_map/all_gather | solution.py:22
  230.7 97.7 %all-to-all-start = ((bf16[192,4,4096]{2,0,1:T(8,128)(2,1)}), bf16[192,4,4096]{2,0,1:T(8,128)(2,1)}, u32[]{:S(2)}, u32[]{:S(2)}) async-start(bf16[192,4,4096]{2,0,1:T(8,128)(2,1)} %bitcast.56), calls=%async_computation | async-start | bytes 12582912 | tf_op jit(solution)/shard_map/all_to_all | solution.py:24
  328.4 22.6 %copy-start.1 = (bf16[192,256]{1,0:T(8,128)(2,1)S(1)}, bf16[192,256]{1,0:T(8,128)(2,1)}, u32[]{:S(2)}) copy-start(bf16[192,256]{1,0:T(8,128)(2,1)} %param.2) | copy-start | bytes 294916
Sparse Core Ops, SparseCore 0:
  12.1 76.5 all-reduce.3
  159.7 64.6 all-gather.4
  226.2 100.3 all-gather.2
where the time goes:
time: 358 us
  waiting for transfers between devices  234 us (65%)
  other arithmetic  54.8 us (15%)
  matrix products  34.6 us (10%)
  between operations  15.2 us (4%)
  local copies, waits for them, and re-layouts  13.4 us (4%)
  starting transfers between devices  5.64 us (2%)
    all_gather x1, waiting for transfers between devices, per_device(): mine = lax.all_gather(residual, 'days', axis=0, tiled=True)  90.4 us
    psum x1, waiting for transfers between devices, per_device(): gram, cross = lax.psum((gram, cross), 'days')  76.7 us
    all_gather x1, waiting for transfers between devices, per_device(): day_block = lax.all_gather(residual, 'assets', axis=1, tiled=True)  64.1 us
    another operation x6, other arithmetic, per_device(): lower = jnp.linalg.cholesky(gram)  34 us
    dot_general x1, matrix products, per_device(): lax.dot_general(mine, columns, (((0,), (0,)), ((), ())), preferred_elemen...  22.6 us
    another operation x4, other arithmetic, per_device(): lax.linalg.triangular_solve(lower, middle, left_side=True, lower=True, tr...  19.8 us
  transfers between devices with their start and end apart: 4, of which 4 were waited for; matrix products, arithmetic and copies ran while one was open for 2% of the time, Pallas kernels for 0%

commit v1 on v0

--- a/solution.py
+++ b/solution.py
@@ -2,6 +2,7 @@
 import jax.numpy as jnp
 from jax import lax
 from jax.sharding import PartitionSpec as P
+from jax.lax import axis_index, ppermute, psum
 
 
 def per_device(factors, returns):
@@ -20,7 +21,19 @@
     fitted = jnp.dot(factors, loadings.astype(jnp.bfloat16), preferred_element_type=jnp.float32)
     residual = (returns.astype(jnp.float32) - fitted).astype(jnp.bfloat16)
     mine = lax.all_gather(residual, "days", axis=0, tiled=True)
-    day_block = lax.all_gather(residual, "assets", axis=1, tiled=True)
+
+    def place_knots_for(inp, axis_tag):
+        num_devices = psum(1, axis_tag)
+        trail = [(pp, (pp + 1) % num_devices) for pp in range(num_devices)]
+        carry_in = [None] * num_devices
+        carry_in[num_devices - 1] = inp
+        for d in range(num_devices - 2, -1, -1):
+            carry_in[d] = ppermute(carry_in[d + 1], axis_tag, perm=trail)
+        found_now = jnp.concatenate(carry_in, axis=1)
+        x_now = axis_index(axis_tag)
+        return jnp.roll(found_now, (x_now + 1) * inp.shape[1], axis=1)
+
+    day_block = place_knots_for(residual, "assets")
     columns = lax.all_to_all(day_block, "days", split_axis=1, concat_axis=0, tiled=True)
     covariance = lax.dot_general(
         mine, columns, (((0,), (0,)), ((), ())), preferred_element_type=jnp.float32

time: 358 us -> 387 us (1.081)
  local copies, waits for them, and re-layouts: 13.4 us -> 43.4 us
  waiting for transfers between devices: 234 us -> 229 us
    ppermute x0 -> x7, waiting for transfers between devices: none -> 92.8 us  [place_knots_for(): carry_in[d] = ppermute(carry_in[d + 1], axis_tag, perm=trail)]
    all_gather x1, waiting for transfers between devices: 90.4 us -> 0.02 us  [per_device(): mine = lax.all_gather(residual, 'days', axis=0, tiled=True)]
    all_gather x1 -> x0, waiting for transfers between devices: 64.1 us -> none  [per_device(): day_block = lax.all_gather(residual, 'assets', axis=1, tiled=True)]
    all_to_all x1, waiting for transfers between devices: 1.8 us -> 59.5 us  [per_device(): lax.all_to_all(day_block, 'days', split_axis=1, concat_axis=0, tiled=True)]
    unnamed x10 -> x45, local copies, waits for them, and re-layouts: 1.84 us -> 31 us
  transfers between devices with their start and end apart: 4 -> 10, of which waited for: 4 -> 9; matrix products, arithmetic and copies ran while one was open for 2% -> 9% of each run, Pallas kernels for 0% -> 0%
where the time goes in v1:
time: 387 us; the launch traced here: 386 us
  waiting for transfers between devices  229 us (59%)
  other arithmetic  54.8 us (14%)
  local copies, waits for them, and re-layouts  43.4 us (11%)
  matrix products  37.6 us (10%)
  between operations  15.6 us (4%)
  starting transfers between devices  5.62 us (1%)
    ppermute x7, waiting for transfers between devices, place_knots_for(): carry_in[d] = ppermute(carry_in[d + 1], axis_tag, perm=trail)  92.8 us
    psum x1, waiting for transfers between devices, per_device(): gram, cross = lax.psum((gram, cross), 'days')  76.7 us
    all_to_all x1, waiting for transfers between devices, per_device(): lax.all_to_all(day_block, 'days', split_axis=1, concat_axis=0, tiled=True)  59.5 us
    another operation x6, other arithmetic, per_device(): lower = jnp.linalg.cholesky(gram)  34 us
    unnamed x45, local copies, waits for them, and re-layouts  31 us
    dot_general x1, matrix products, per_device(): lax.dot_general(mine, columns, (((0,), (0,)), ((), ())), preferred_elemen...  22.6 us
    another operation x4, other arithmetic, per_device(): lax.linalg.triangular_solve(lower, middle, left_side=True, lower=True, tr...  19.8 us
  transfers between devices with their start and end apart: 10, of which 9 were waited for; matrix products, arithmetic and copies ran while one was open for 9% of the time, Pallas kernels for 0%

profile of v1, /device:TPU:0, one launch (start us, length us, event | category | flops | bytes accessed | tf_op | source)
XLA Modules:
  0.0 386.3 jit_solution(2429920080524293062)
XLA Ops:
  7.2 0.0 all-reduce.4.cloned.1.call-start
  7.2 0.8 copy-done
  8.1 0.9 fusion.15
  9.0 2.9 fusion.16
  11.9 0.0 all-gather.2.cloned.1.call-start
  12.0 76.7 %all-reduce.4.cloned.1.call-done = (f32[256,2048]{1,0:T(8,128)}, f32[256,256]{0,1:T(8,128)}) async-done(((f32[256,2048]{1,0:T(8,128)}, f32[256,256]{0,1:T(8,128)}), (f32[256,2048]{1,0:T(8,128)}, f32[256,256]{0,1:T(8,128)})) %all-reduce.4.cloned.1.call-update) | async-done | bytes 2359312 | tf_op jit(solution)/shard_map/psum | solution.py:15
  88.7 1.1 copy.12
  89.8 1.0 fusion.5
  90.8 11.7 %cholesky.50 = f32[128,128]{1,0:T(8,128)S(1)} custom-call(f32[128,128]{1,0:T(8,128)S(1)} %cholesky.118), custom_call_target="Cholesky" | custom-call | tf_op jit(solution)/shard_map/jit(cholesky)/cholesky | solution.py:16
  102.5 9.8 %custom-call.16 = f32[1,128,128]{1,2,0:T(8,128)S(1)} custom-call(f32[1,128,128]{2,1,0:T(8,128)S(1)} %get-tuple-element.25), custom_call_target="InvertDiagBlocksLowerTriangular" | custom-call | tf_op jit(solution)/shard_map/jit(cholesky)/cholesky | solution.py:16
  112.4 0.2 constant_dynamic-update-slice_fusion.16
  112.6 0.3 convolution_subtract_fusion.2
  112.8 11.7 %cholesky.105 = f32[128,128]{1,0:T(8,128)S(1)} custom-call(f32[128,128]{1,0:T(8,128)S(1)} %convolution_subtract_fusion.2), custom_call_target="Cholesky" | custom-call | tf_op jit(solution)/shard_map/jit(cholesky)/cholesky | solution.py:16
  124.6 0.6 compare_reduce_fusion
  126.6 0.1 triangular_solve.66
  126.6 4.1 %while.1 = (s32[]{:T(128)}, f32[256,256]{1,0:T(8,128)S(1)}, s32[2,2]{1,0:T(2,128)S(1)}, f32[2,128,128]{2,1,0:T(8,128)S(1)}, s32[]{:T(128)}) while((s32[]{:T(128)}, f32[256,256]{1,0:T(8,128)S(1)}, s32[2,2]{1,0:T(2,128)S(1)}, f32[2,128,128]{2,1,0:T(8,128)S(1)}, s32[]{:T(128)}) %tuple.27), condition=%wide.while_cond, body=%wide.while_body.sunk | while | flops 2 | bytes 131189 | solution.py:18
  126.8 0.6 fusion.32
  127.4 1.4 bitcast_dynamic-update-slice_fusion.2
  128.8 0.6 fusion.32
  129.4 1.4 bitcast_dynamic-update-slice_fusion.2
  130.8 19.7 %custom-call.17 = f32[2,128,128]{1,2,0:T(8,128)S(1)} custom-call(f32[2,128,128]{2,1,0:T(8,128)S(1)} %get-tuple-element.9), custom_call_target="InvertDiagBlocksLowerTriangular" | custom-call | tf_op jit(solution)/shard_map/triangular_solve | solution.py:18
  150.5 2.3 fusion.2
  152.7 2.2 convolution_subtract_fusion.1
  155.0 1.1 fusion.11
  156.0 1.0 fusion.10
  157.1 1.0 convolution_subtract_fusion
  158.1 1.0 fusion.9
  159.1 0.1 pad_maximum_fusion
  159.3 2.1 fusion.1
  161.4 0.1 collective-permute-start
  161.5 13.2 %collective-permute-done = bf16[192,2048]{1,0:T(8,128)(2,1)S(1)} collective-permute-done((bf16[192,2048]{1,0:T(8,128)(2,1)S(1)}, bf16[192,2048]{1,0:T(8,128)(2,1)S(1)}, u32[]{:S(2)}, u32[]{:S(2)}) %collective-permute-start) | collective-permute-done | bytes 786464 | tf_op jit(solution)/shard_map/ppermute | solution.py:31
  174.7 0.9 copy-done.5
  175.5 13.2 %collective-permute-done.1 = bf16[192,2048]{1,0:T(8,128)(2,1)S(1)} collective-permute-done((bf16[192,2048]{1,0:T(8,128)(2,1)S(1)}, bf16[192,2048]{1,0:T(8,128)(2,1)S(1)}, u32[]{:S(2)}, u32[]{:S(2)}) %collective-permute-start.1) | collective-permute-done | bytes 786464 | tf_op jit(solution)/shard_map/ppermute | solution.py:31
  188.8 0.9 copy-done.7
  189.7 13.2 %collective-permute-done.2 = bf16[192,2048]{1,0:T(8,128)(2,1)S(1)} collective-permute-done((bf16[192,2048]{1,0:T(8,128)(2,1)S(1)}, bf16[192,2048]{1,0:T(8,128)(2,1)S(1)}, u32[]{:S(2)}, u32[]{:S(2)}) %collective-permute-start.2) | collective-permute-done | bytes 786464 | tf_op jit(solution)/shard_map/ppermute | solution.py:31
  202.9 0.9 copy-done.9
  203.8 13.2 %collective-permute-done.3 = bf16[192,2048]{1,0:T(8,128)(2,1)S(1)} collective-permute-done((bf16[192,2048]{1,0:T(8,128)(2,1)S(1)}, bf16[192,2048]{1,0:T(8,128)(2,1)S(1)}, u32[]{:S(2)}, u32[]{:S(2)}) %collective-permute-start.3) | collective-permute-done | bytes 786464 | tf_op jit(solution)/shard_map/ppermute | solution.py:31
  217.0 0.9 copy-done.11
  217.9 13.2 %collective-permute-done.4 = bf16[192,2048]{1,0:T(8,128)(2,1)S(1)} collective-permute-done((bf16[192,2048]{1,0:T(8,128)(2,1)S(1)}, bf16[192,2048]{1,0:T(8,128)(2,1)S(1)}, u32[]{:S(2)}, u32[]{:S(2)}) %collective-permute-start.4) | collective-permute-done | bytes 786464 | tf_op jit(solution)/shard_map/ppermute | solution.py:31
  231.1 0.9 copy-done.13
  232.0 13.3 %collective-permute-done.5 = bf16[192,2048]{1,0:T(8,128)(2,1)} collective-permute-done((bf16[192,2048]{1,0:T(8,128)(2,1)S(1)}, bf16[192,2048]{1,0:T(8,128)(2,1)}, u32[]{:S(2)}, u32[]{:S(2)}) %collective-permute-start.5) | collective-permute-done | bytes 786464 | tf_op jit(solution)/shard_map/ppermute | solution.py:31
  245.4 13.4 %collective-permute-done.6 = bf16[192,2048]{1,0:T(8,128)(2,1)} collective-permute-done((bf16[192,2048]{1,0:T(8,128)(2,1)}, bf16[192,2048]{1,0:T(8,128)(2,1)}, u32[]{:S(2)}, u32[]{:S(2)}) %collective-permute-start.6) | collective-permute-done | bytes 786464 | tf_op jit(solution)/shard_map/ppermute | solution.py:31
  258.8 2.1 constant_dynamic-update-slice_fusion.15
  260.9 2.1 constant_dynamic-update-slice_fusion.14
  263.0 2.1 constant_dynamic-update-slice_fusion.13
  265.1 2.1 constant_dynamic-update-slice_fusion.12
  267.2 2.1 constant_dynamic-update-slice_fusion.11
  269.3 2.1 constant_dynamic-update-slice_fusion.10
  271.4 2.1 constant_dynamic-update-slice_fusion.9
  273.4 2.1 constant_dynamic-update-slice_fusion.8
  275.5 2.1 constant_dynamic-update-slice_fusion.7
  277.6 2.1 constant_dynamic-update-slice_fusion.6
  279.7 1.0 constant_dynamic-update-slice_fusion.5
  280.7 1.0 constant_dynamic-update-slice_fusion.4
  281.6 1.0 constant_dynamic-update-slice_fusion.3
  282.6 1.0 constant_dynamic-update-slice_fusion.2
  283.6 1.0 constant_dynamic-update-slice_fusion.1
  284.5 1.0 constant_dynamic-update-slice_fusion
  285.5 3.2 constant_dynamic-slice_fusion.1
  288.7 3.1 copy.17
  291.8 5.5 %all-to-all-start = ((bf16[192,4,4096]{2,0,1:T(8,128)(2,1)}), bf16[192,4,4096]{2,0,1:T(8,128)(2,1)}, u32[]{:S(2)}, u32[]{:S(2)}) async-start(bf16[192,4,4096]{2,0,1:T(8,128)(2,1)} %bitcast.56), calls=%async_computation | async-start | bytes 12582912 | tf_op jit(solution)/shard_map/all_to_all | solution.py:37
  297.3 0.0 all-gather.2.cloned.1.call-done
  297.3 59.5 %all-to-all-done = bf16[192,4,4096]{2,0,1:T(8,128)(2,1)} async-done(((bf16[192,4,4096]{2,0,1:T(8,128)(2,1)}), bf16[192,4,4096]{2,0,1:T(8,128)(2,1)}, u32[]{:S(2)}, u32[]{:S(2)}) %all-to-all-start) | async-done | bytes 6291488 | tf_op jit(solution)/shard_map/all_to_all | solution.py:37
  356.8 22.6 %convolution_multiply_fusion = f32[2048,4096]{1,0:T(8,128)} fusion(bf16[768,2048]{1,0:T(8,128)(2,1)} %all-gather.2.cloned.1.call-done, bf16[768,4096]{1,0:T(8,128)(2,1)} %bitcast.7), kind=kOutput, calls=%fused_computation.2 | convolution fusion | flops 12893290496 | bytes 42991616 | tf_op jit(solution)/shard_map/dot_general | solution.py:38
  (41 shorter events, 0.3 us)
Async XLA Ops:
  7.2 0.9 copy-start
  7.2 81.5 %all-reduce.4.cloned.1.call-start = ((), (), s32[]{:S(2)}) async-start(), calls=%async_computation.2 | async-start | bytes 4718592 | tf_op jit(solution)/shard_map/psum | solution.py:15
  11.9 285.4 %all-gather.2.cloned.1.call-start = ((), (), s32[]{:S(2)}) async-start(), calls=%async_computation.1 | async-start | bytes 3932160 | tf_op jit(solution)/shard_map/all_gather | solution.py:23
  159.3 124.3 %copy-start.4 = (f32[256,2048]{1,0:T(8,128)}, f32[256,2048]{1,0:T(8,128)S(1)}, u32[]{:S(2)}) copy-start(f32[256,2048]{1,0:T(8,128)S(1)} %pad_maximum_fusion) | copy-start | bytes 6291460
  161.4 83.9 %copy-start.2 = (bf16[192,2048]{1,0:T(8,128)(2,1)}, bf16[192,2048]{1,0:T(8,128)(2,1)S(1)}, u32[]{:S(2)}) copy-start(bf16[192,2048]{1,0:T(8,128)(2,1)S(1)} %fusion.1) | copy-start | bytes 2359300
  161.4 13.3 %collective-permute-start = (bf16[192,2048]{1,0:T(8,128)(2,1)S(1)}, bf16[192,2048]{1,0:T(8,128)(2,1)S(1)}, u32[]{:S(2)}, u32[]{:S(2)}) collective-permute-start(bf16[192,2048]{1,0:T(8,128)(2,1)S(1)} %fusion.1), channel_id=1, source_target_pairs={{0,1},{1,2},{2,3},{3,4},{4,5},{5,6},{6,7},{7,0},{8,9},{9,10},{10,1... | collective-permute-start | bytes 2359304 | tf_op jit(solution)/shard_map/ppermute | solution.py:31
  174.7 0.9 copy-start.5
  175.5 13.2 %collective-permute-start.1 = (bf16[192,2048]{1,0:T(8,128)(2,1)S(1)}, bf16[192,2048]{1,0:T(8,128)(2,1)S(1)}, u32[]{:S(2)}, u32[]{:S(2)}) collective-permute-start(bf16[192,2048]{1,0:T(8,128)(2,1)S(1)} %collective-permute-done), channel_id=1, source_target_pairs={{0,1},{1,2},{2,3},{3,4},{4,5},{5,6},{6,7},{7,0},{8,9},{9,10},{10,1... | collective-permute-start | bytes 2359304 | tf_op jit(solution)/shard_map/ppermute | solution.py:31
  188.8 0.9 copy-start.7
  189.7 13.2 %collective-permute-start.2 = (bf16[192,2048]{1,0:T(8,128)(2,1)S(1)}, bf16[192,2048]{1,0:T(8,128)(2,1)S(1)}, u32[]{:S(2)}, u32[]{:S(2)}) collective-permute-start(bf16[192,2048]{1,0:T(8,128)(2,1)S(1)} %collective-permute-done.1), channel_id=1, source_target_pairs={{0,1},{1,2},{2,3},{3,4},{4,5},{5,6},{6,7},{7,0},{8,9},{9,10},{10,1... | collective-permute-start | bytes 2359304 | tf_op jit(solution)/shard_map/ppermute | solution.py:31
  202.9 0.9 copy-start.9
  203.8 13.2 %collective-permute-start.3 = (bf16[192,2048]{1,0:T(8,128)(2,1)S(1)}, bf16[192,2048]{1,0:T(8,128)(2,1)S(1)}, u32[]{:S(2)}, u32[]{:S(2)}) collective-permute-start(bf16[192,2048]{1,0:T(8,128)(2,1)S(1)} %collective-permute-done.2), channel_id=1, source_target_pairs={{0,1},{1,2},{2,3},{3,4},{4,5},{5,6},{6,7},{7,0},{8,9},{9,10},{10,1... | collective-permute-start | bytes 2359304 | tf_op jit(solution)/shard_map/ppermute | solution.py:31
  217.0 0.9 copy-start.11
  217.9 13.2 %collective-permute-start.4 = (bf16[192,2048]{1,0:T(8,128)(2,1)S(1)}, bf16[192,2048]{1,0:T(8,128)(2,1)S(1)}, u32[]{:S(2)}, u32[]{:S(2)}) collective-permute-start(bf16[192,2048]{1,0:T(8,128)(2,1)S(1)} %collective-permute-done.3), channel_id=1, source_target_pairs={{0,1},{1,2},{2,3},{3,4},{4,5},{5,6},{6,7},{7,0},{8,9},{9,10},{10,1... | collective-permute-start | bytes 2359304 | tf_op jit(solution)/shard_map/ppermute | solution.py:31
  231.1 0.9 copy-start.13
  232.0 13.3 %collective-permute-start.5 = (bf16[192,2048]{1,0:T(8,128)(2,1)S(1)}, bf16[192,2048]{1,0:T(8,128)(2,1)}, u32[]{:S(2)}, u32[]{:S(2)}) collective-permute-start(bf16[192,2048]{1,0:T(8,128)(2,1)S(1)} %collective-permute-done.4), channel_id=1, source_target_pairs={{0,1},{1,2},{2,3},{3,4},{4,5},{5,6},{6,7},{7,0},{8,9},{9,10},{10,1... | collective-permute-start | bytes 2359304 | tf_op jit(solution)/shard_map/ppermute | solution.py:31
  245.3 13.5 %collective-permute-start.6 = (bf16[192,2048]{1,0:T(8,128)(2,1)}, bf16[192,2048]{1,0:T(8,128)(2,1)}, u32[]{:S(2)}, u32[]{:S(2)}) collective-permute-start(bf16[192,2048]{1,0:T(8,128)(2,1)} %collective-permute-done.5), channel_id=1, source_target_pairs={{0,1},{1,2},{2,3},{3,4},{4,5},{5,6},{6,7},{7,0},{8,9},{9,10},{10,1... | collective-permute-start | bytes 2359304 | tf_op jit(solution)/shard_map/ppermute | solution.py:31
  245.3 34.4 %copy-start.14 = (bf16[192,2048]{1,0:T(8,128)(2,1)S(1)}, bf16[192,2048]{1,0:T(8,128)(2,1)}, u32[]{:S(2)}) copy-start(bf16[192,2048]{1,0:T(8,128)(2,1)} %copy-done.13) | copy-start | bytes 2359300
  245.3 35.3 %copy-start.12 = (bf16[192,2048]{1,0:T(8,128)(2,1)S(1)}, bf16[192,2048]{1,0:T(8,128)(2,1)}, u32[]{:S(2)}) copy-start(bf16[192,2048]{1,0:T(8,128)(2,1)} %copy-done.11) | copy-start | bytes 2359300
  245.3 36.3 %copy-start.10 = (bf16[192,2048]{1,0:T(8,128)(2,1)S(1)}, bf16[192,2048]{1,0:T(8,128)(2,1)}, u32[]{:S(2)}) copy-start(bf16[192,2048]{1,0:T(8,128)(2,1)} %copy-done.9) | copy-start | bytes 2359300
  245.4 37.2 %copy-start.8 = (bf16[192,2048]{1,0:T(8,128)(2,1)S(1)}, bf16[192,2048]{1,0:T(8,128)(2,1)}, u32[]{:S(2)}) copy-start(bf16[192,2048]{1,0:T(8,128)(2,1)} %copy-done.7) | copy-start | bytes 2359300
  245.4 38.2 %copy-start.6 = (bf16[192,2048]{1,0:T(8,128)(2,1)S(1)}, bf16[192,2048]{1,0:T(8,128)(2,1)}, u32[]{:S(2)}) copy-start(bf16[192,2048]{1,0:T(8,128)(2,1)} %copy-done.5) | copy-start | bytes 2359300
  245.4 39.1 %copy-start.3 = (bf16[192,2048]{1,0:T(8,128)(2,1)S(1)}, bf16[192,2048]{1,0:T(8,128)(2,1)}, u32[]{:S(2)}) copy-start(bf16[192,2048]{1,0:T(8,128)(2,1)} %copy-done.2) | copy-start | bytes 2359300
  291.8 65.0 %all-to-all-start = ((bf16[192,4,4096]{2,0,1:T(8,128)(2,1)}), bf16[192,4,4096]{2,0,1:T(8,128)(2,1)}, u32[]{:S(2)}, u32[]{:S(2)}) async-start(bf16[192,4,4096]{2,0,1:T(8,128)(2,1)} %bitcast.56), calls=%async_computation | async-start | bytes 12582912 | tf_op jit(solution)/shard_map/all_to_all | solution.py:37
  356.8 22.6 %copy-start.1 = (bf16[192,256]{1,0:T(8,128)(2,1)S(1)}, bf16[192,256]{1,0:T(8,128)(2,1)}, u32[]{:S(2)}) copy-start(bf16[192,256]{1,0:T(8,128)(2,1)} %param.2) | copy-start | bytes 294916
Sparse Core Ops, SparseCore 0:
  12.1 76.5 all-reduce.3
  245.4 44.1 all-gather.1
